TPU v7x, 128 devices: a whole 4x4x4 slice. The times are simulated.
128 devices in a mesh: rcv: 16 (over x_hi, y, core), src: 8 (over z, x_lo).
Axes of the slice: x: 4 (x_hi: 2, x_lo: 2; x = x_hi * 2 + x_lo), y: 4, z: 4, core: 2. Of those that a mesh axis runs over, the one named last changes fastest.
Arguments:
- kernel_codes: bfloat16 [2, 8192, 65536], P(None, 'rcv', 'src'), may hold values from -128 to 127
- kernel_exps: int32 [8192, 512], P('rcv', 'src'), may hold values from -17 to -14
- wavefield: bfloat16 [2, 65536, 128], P(None, 'src', 'rcv'), may hold values from -6 to 6
- observed: bfloat16 [2, 8192, 128], P(None, 'rcv'), may hold values from -6 to 6
- receiver_mask: int32 [8192], P('rcv'), may hold values 0 or 1
Outputs:
- residual: bfloat16 [2, 8192, 128], P(None, 'rcv', 'src')
- gradient: bfloat16 [2, 65536, 128], P(None, 'src', 'rcv')
All inputs are finite; a program needn't handle non-finite values. No bound on the sum of `receiver_mask` on one device may be relied on, other than what follows from the above.
Results may differ from a plain program's by a relative error of at most 0.0049.
Values may be sent and summed in bfloat16 or wider, within the bound.
No kernel may reach another device: no remote copies, remote signals or barrier semaphores. Data moves between devices by JAX's collectives and lax.ppermute only.
A program may use at most 128 MiB of HBM per device.

v0:
```python
import jax
import jax.numpy as jnp
from jax import lax
from jax.sharding import PartitionSpec as P

EXP_BLOCK = 128


def decode(codes, exps):
    rows = codes.shape[1]
    cols = codes.shape[2]
    scale = jnp.exp2(exps.astype(jnp.float32))[:, :, None]

    def widen(values):
        blocks = values.reshape(rows, cols // EXP_BLOCK, EXP_BLOCK).astype(jnp.float32) * scale
        return blocks.reshape(rows, cols).astype(jnp.bfloat16)

    return jnp.concatenate([widen(codes[0]), widen(codes[1])], axis=0)


def body(kernel_codes, kernel_exps, wavefield, observed, receiver_mask):
    rows = kernel_codes.shape[1]
    n_src = lax.axis_size("src")
    stacked = decode(kernel_codes, kernel_exps)
    piece = lax.all_gather(wavefield, "rcv", axis=2, tiled=True)
    span = piece.shape[2]
    joined = jnp.concatenate([piece[0], piece[1]], axis=1)
    prod = jnp.dot(stacked, joined, preferred_element_type=jnp.float32)
    pred_real = prod[:rows, :span] - prod[rows:, span:]
    pred_imag = prod[:rows, span:] + prod[rows:, :span]
    partial_pred = jnp.stack([pred_real, pred_imag])
    width = partial_pred.shape[2]
    share_cols = width // n_src
    live = receiver_mask.astype(jnp.float32)[None, :, None]
    predicted = lax.psum(partial_pred, "src")
    resid = (live * (predicted - observed.astype(jnp.float32))).astype(jnp.bfloat16)
    own_resid = lax.dynamic_slice_in_dim(resid, lax.axis_index("src") * share_cols, share_cols, 2)
    left = jnp.concatenate([resid[0], resid[1]], axis=0)
    right = jnp.concatenate([resid[1], -resid[0]], axis=0)
    grad_real = lax.dot_general(
        stacked, left, (((0,), (0,)), ((), ())), preferred_element_type=jnp.float32
    )
    grad_imag = lax.dot_general(
        stacked, right, (((0,), (0,)), ((), ())), preferred_element_type=jnp.float32
    )
    summed = lax.psum_scatter(
        jnp.stack([grad_real, grad_imag]), "rcv", scatter_dimension=2, tiled=True
    )
    gradient = summed.astype(jnp.bfloat16)
    return (own_resid, gradient)


def solution(mesh):
    in_specs = (
        P(None, "rcv", "src"),
        P("rcv", "src"),
        P(None, "src", "rcv"),
        P(None, "rcv", None),
        P("rcv"),
    )
    out_specs = (P(None, "rcv", "src"), P(None, "src", "rcv"))
    return jax.shard_map(body, mesh=mesh, in_specs=in_specs, out_specs=out_specs, check_vma=False)
```

profile of v0, /device:TPU:0, one launch (start us, length us, event | category | flops | bytes accessed | tf_op | source)
XLA Modules:
  0.0 313.3 jit_solution(1897431621627236321)
XLA Ops:
  7.2 0.0 all-gather.2.cloned.1.call-start
  7.2 0.7 all-gather.2.cloned.1.call-update
  7.9 0.0 all-reduce.4.cloned.1.call-start
  7.9 0.9 multiply_exponential_fusion
  8.9 0.1 copy.10
  9.0 4.6 %mul.30 = f32[512,64,128]{2,1,0:T(8,128)S(1)} broadcast(f32[512,64]{1,0:T(8,128)S(1)} %copy.10), dimensions={0,1} | broadcast | bytes 16908288 | tf_op jit(solution)/shard_map/mul | solution.py:15
  13.6 18.3 %fusion = (bf16[512,8192]{1,0:T(8,128)(2,1)}, bf16[512,8192]{1,0:T(8,128)(2,1)}) fusion(f32[64,8,64,128]{3,2,1,0:T(8,128)S(1)} %bitcast.33, bf16[2,512,8192]{2,1,0:T(8,128)(2,1)} %param.5), kind=kLoop, calls=%fused_computation.2 | loop fusion | flops 25165824 | bytes 50331648 | tf_op jit(solution)/shard_map/convert_element_type | solution.py:16
  32.0 35.8 %all-gather.2.cloned.1.call-done = bf16[2,8192,128]{1,2,0:T(8,128)(2,1)} async-done(((bf16[2,8192,8]{1,2,0:T(8,128)(2,1)}), bf16[2,8192,128]{1,2,0:T(8,128)(2,1)}) %all-gather.2.cloned.1.call-update) | async-done | bytes 4194320 | tf_op jit(solution)/shard_map/all_gather | solution.py:25
  67.7 0.0 copy-start
  67.7 4.1 %slice_bitcast_fusion.1 = (bf16[8192,128]{0,1:T(8,128)(2,1)S(1)}, bf16[8192,128]{0,1:T(8,128)(2,1)}) fusion(bf16[2,8192,128]{1,2,0:T(8,128)(2,1)} %all-gather.2.cloned.1.call-done), kind=kLoop, calls=%fused_computation.13 | loop fusion | bytes 8388608 | tf_op jit(solution)/shard_map/squeeze | solution.py:27
  71.8 1.3 copy-done
  73.1 0.0 copy-start.2
  73.1 0.0 copy-start.3
  73.1 0.0 copy-start.1
  73.1 9.5 %fusion.2 = f32[1024,256]{1,0:T(8,128)} fusion(bf16[512,8192]{1,0:T(8,128)(2,1)} %get-tuple-element.7, bf16[512,8192]{1,0:T(8,128)(2,1)S(1)} %copy-done, bf16[8192,128]{0,1:T(8,128)(2,1)} %get-tuple-element.9, bf16[8192,128]{0,1:T(8,128)(2,1)S(1)} %get-tuple-element.8), kind=kOutput, calls=%fused_computation.8 | convolution fusion | flops 4336910336 | bytes 22020096 | tf_op jit(solution)/shard_map/dot_general | solution.py:28
  82.7 1.2 fusion.7
  83.9 0.8 pad_maximum_fusion.5
  84.7 0.0 all-reduce.4.cloned.1.call-update
  84.8 0.0 copy-done.2
  84.8 0.0 copy-done.3
  84.8 0.6 dynamic-slice
  86.1 73.1 %all-reduce.4.cloned.1.call-done = f32[2,512,128]{2,1,0:T(8,128)} async-done(((f32[2,512,128]{2,1,0:T(8,128)}), f32[2,512,128]{2,1,0:T(8,128)}) %all-reduce.4.cloned.1.call-update) | async-done | bytes 524304 | tf_op jit(solution)/shard_map/psum | solution.py:35
  159.2 0.0 copy-done.1
  159.2 0.0 slice-start
  159.2 0.0 slice-start.2
  159.2 1.3 multiply_convert_fusion
  160.6 0.0 slice-start.1
  160.6 0.0 slice-start.3
  160.6 10.2 %convolution_bitcast_fusion.1 = f32[1,8192,128]{2,1,0:T(8,128)} fusion(bf16[512,8192]{1,0:T(8,128)(2,1)} %get-tuple-element.7, bf16[512,8192]{1,0:T(8,128)(2,1)} %get-tuple-element.6, bf16[512,128]{1,0:T(8,128)(2,1)S(1)} %get-tuple-element.13, bf16[512,128]{1,0:T(8,128)(2,1)S(1)} %get-tuple-element.12), kind=kOutput, calls=%fused_computation.6 | convolution fusion | flops 2181562368 | bytes 21233664 | tf_op jit(solution)/shard_map/dot_general | solution.py:40
  170.8 0.0 slice-done
  170.8 0.0 slice-done.2
  170.9 0.0 slice-done.1
  170.9 0.9 slice-done.3
  171.7 6.3 %convolution_bitcast_fusion = f32[1,8192,128]{2,1,0:T(8,128)} fusion(bf16[512,8192]{1,0:T(8,128)(2,1)S(1)} %bitcast.37, bf16[512,8192]{1,0:T(8,128)(2,1)S(1)} %bitcast.35, bf16[512,128]{1,0:T(8,128)(2,1)S(1)} %fusion.17, bf16[512,128]{1,0:T(8,128)(2,1)S(1)} %get-tuple-element.13), kind=kOutput, calls=%fused_computation.5 | convolution fusion | flops 2181562368 | bytes 21233664 | tf_op jit(solution)/shard_map/dot_general | solution.py:43
  178.0 7.2 %pad_maximum_fusion.1 = f32[2,8192,128]{2,1,0:T(8,128)} fusion(f32[1,8192,128]{2,1,0:T(8,128)} %convolution_bitcast_fusion, f32[1,8192,128]{2,1,0:T(8,128)} %convolution_bitcast_fusion.1), kind=kLoop, calls=%fused_computation.7 | loop fusion | flops 2097152 | bytes 16777216 | tf_op jit(solution)/shard_map/stack | solution.py:47
  185.2 13.2 %copy.11 = f32[2,8192,128]{1,0,2:T(2,128)} copy(f32[2,8192,128]{2,1,0:T(8,128)} %pad_maximum_fusion.1) | data formatting | bytes 16777216 | tf_op jit(solution)/shard_map/stack | solution.py:47
  198.4 105.1 %all-reduce.5 = bf16[2,8192,128]{1,0,2:T(2,128)(2,1)} all-reduce(f32[2,8192,128]{1,0,2:T(2,128)} %copy.11), channel_id=2, replica_groups=mesh['rcv'=16,'src'=8] {'rcv'}, use_global_device_ids=true, to_apply=%region_1.0.clone | all-reduce | flops 2097152 | bytes 12582912
  303.6 1.1 dynamic-slice_convert_fusion
  304.7 0.9 copy.13
  305.6 0.1 constant_dynamic-slice_fusion
  305.7 0.7 copy.12
  (5 shorter events, 0.0 us)
Async XLA Ops:
  7.2 60.6 %all-gather.2.cloned.1.call-start = ((), (), s32[]{:S(2)}) async-start(), calls=%async_computation | async-start | bytes 4456448 | tf_op jit(solution)/shard_map/all_gather | solution.py:25
  7.9 151.3 %all-reduce.4.cloned.1.call-start = ((), (), s32[]{:S(2)}) async-start(), calls=%async_computation.1 | async-start | bytes 1048576 | tf_op jit(solution)/shard_map/psum | solution.py:35
  67.7 5.4 %copy-start = (bf16[512,8192]{1,0:T(8,128)(2,1)S(1)}, bf16[512,8192]{1,0:T(8,128)(2,1)}, u32[]{:S(2)}) copy-start(bf16[512,8192]{1,0:T(8,128)(2,1)} %get-tuple-element.6) | copy-start | bytes 25165828
  73.1 11.7 %copy-start.2 = (s32[512]{0:T(512)S(1)}, s32[512]{0:T(512)}, u32[]{:S(2)}) copy-start(s32[512]{0:T(512)} %param.9) | copy-start | bytes 6148
  73.1 11.7 %copy-start.3 = (u32[128]{0:T(128)S(1)}, u32[128]{0:T(128)}, u32[]{:S(2)}) copy-start(u32[128]{0:T(128)} %constant.15) | copy-start | bytes 1540
  73.1 86.1 %copy-start.1 = (bf16[2,512,128]{2,1,0:T(8,128)(2,1)S(1)}, bf16[2,512,128]{2,1,0:T(8,128)(2,1)}, u32[]{:S(2)}) copy-start(bf16[2,512,128]{2,1,0:T(8,128)(2,1)} %param.8) | copy-start | bytes 786436
  159.2 11.6 %slice-start = ((s8[8388608]{0:T(1024)(128)(4,1)}), s8[4194304]{0:T(1024)(128)(4,1)S(1)}, s32[]{:S(2)}) async-start(s8[8388608]{0:T(1024)(128)(4,1)} %bitcast.34), calls=%async_computation.2 | async-start | bytes 8388608
  159.2 11.6 %slice-start.2 = ((s8[8388608]{0:T(1024)(128)(4,1)}), s8[4194304]{0:T(1024)(128)(4,1)S(1)}, s32[]{:S(2)}) async-start(s8[8388608]{0:T(1024)(128)(4,1)} %bitcast.36), calls=%async_computation.4 | async-start | bytes 8388608
  160.6 10.3 %slice-start.1 = ((s8[8388608]{0:T(1024)(128)(4,1)}), s8[4194304]{0:T(1024)(128)(4,1)S(1)}, s32[]{:S(2)}) async-start(s8[8388608]{0:T(1024)(128)(4,1)} %bitcast.34), calls=%async_computation.3 | async-start | bytes 8388608
  160.6 11.1 %slice-start.3 = ((s8[8388608]{0:T(1024)(128)(4,1)}), s8[4194304]{0:T(1024)(128)(4,1)S(1)}, s32[]{:S(2)}) async-start(s8[8388608]{0:T(1024)(128)(4,1)} %bitcast.36), calls=%async_computation.5 | async-start | bytes 8388608
Sparse Core Ops, SparseCore 0:
  10.5 57.1 all-gather.1
  84.9 74.2 all-reduce.3
where the time goes:
time: 314 us; the launch traced here: 313 us
  waiting for transfers between devices  110 us (35%)
  blocking collectives  105 us (33%)
  other arithmetic  29.9 us (10%)
  local copies, waits for them, and re-layouts  27.7 us (9%)
  matrix products  26 us (8%)
  between operations  14.8 us (5%)
    unnamed x1, blocking collectives  105 us
    psum x1, waiting for transfers between devices, body(): predicted = lax.psum(partial_pred, 'src')  73.1 us
    all_gather x1, waiting for transfers between devices, body(): piece = lax.all_gather(wavefield, 'rcv', axis=2, tiled=True)  35.8 us
    convert_element_type x1, other arithmetic, widen(): return blocks.reshape(rows, cols).astype(jnp.bfloat16)  18.3 us
    another operation x1, local copies, waits for them, and re-layouts, body(): jnp.stack([grad_real, grad_imag])  13.2 us
    dot_general x1, matrix products, body(): lax.dot_general(stacked, left, (((0,), (0,)), ((), ())), preferred_elemen...  10.2 us
    dot_general x1, matrix products, body(): prod = jnp.dot(stacked, joined, preferred_element_type=jnp.float32)  9.54 us
    another operation x1, other arithmetic, body(): jnp.stack([grad_real, grad_imag])  7.24 us
  transfers between devices with their start and end apart: 2, of which 2 were waited for; matrix products, arithmetic and copies ran while one was open for 8% of the time, Pallas kernels for 0%

commit v1 on v0

--- a/solution.py
+++ b/solution.py
@@ -32,7 +32,8 @@
     width = partial_pred.shape[2]
     share_cols = width // n_src
     live = receiver_mask.astype(jnp.float32)[None, :, None]
-    predicted = lax.psum(partial_pred, "src")
+    recast_the_plate = lambda u_in, axis_id: lax.all_gather(u_in, axis_id).sum(axis=0)
+    predicted = recast_the_plate(partial_pred, "src")
     resid = (live * (predicted - observed.astype(jnp.float32))).astype(jnp.bfloat16)
     own_resid = lax.dynamic_slice_in_dim(resid, lax.axis_index("src") * share_cols, share_cols, 2)
     left = jnp.concatenate([resid[0], resid[1]], axis=0)

time: 314 us -> 332 us (1.057)
  waiting for transfers between devices: 110 us -> 124 us
    all_gather x0 -> x1, waiting for transfers between devices: none -> 87.7 us  [body(): lax.all_gather(u_in, axis_id).sum(axis=0)]
    psum x1 -> x0, waiting for transfers between devices: 73.1 us -> none  [body(): predicted = lax.psum(partial_pred, 'src')]
  transfers between devices with their start and end apart: 2 -> 2, of which waited for: 2 -> 2; matrix products, arithmetic and copies ran while one was open for 8% -> 7% of each run, Pallas kernels for 0% -> 0%
where the time goes in v1:
time: 332 us; the launch traced here: 331 us
  waiting for transfers between devices  124 us (37%)
  blocking collectives  106 us (32%)
  other arithmetic  31.2 us (9%)
  local copies, waits for them, and re-layouts  28.9 us (9%)
  matrix products  25.8 us (8%)
  between operations  14.8 us (4%)
    unnamed x1, blocking collectives  106 us
    all_gather x1, waiting for transfers between devices, body(): lax.all_gather(u_in, axis_id).sum(axis=0)  87.7 us
    all_gather x1, waiting for transfers between devices, body(): piece = lax.all_gather(wavefield, 'rcv', axis=2, tiled=True)  35.8 us
    convert_element_type x1, other arithmetic, widen(): return blocks.reshape(rows, cols).astype(jnp.bfloat16)  18.3 us
    another operation x1, local copies, waits for them, and re-layouts, body(): jnp.stack([grad_real, grad_imag])  13.2 us
    dot_general x1, matrix products, body(): lax.dot_general(stacked, left, (((0,), (0,)), ((), ())), preferred_elemen...  9.97 us
    dot_general x1, matrix products, body(): prod = jnp.dot(stacked, joined, preferred_element_type=jnp.float32)  9.54 us
    another operation x1, other arithmetic, body(): jnp.stack([grad_real, grad_imag])  7.24 us
  transfers between devices with their start and end apart: 2, of which 2 were waited for; matrix products, arithmetic and copies ran while one was open for 7% of the time, Pallas kernels for 0%

profile of v1, /device:TPU:0, one launch (start us, length us, event | category | flops | bytes accessed | tf_op | source)
XLA Modules:
  0.0 331.0 jit_solution(6209952137003832848)
XLA Ops:
  7.2 0.0 all-gather.4.cloned.1.call-start
  7.2 0.7 all-gather.4.cloned.1.call-update
  7.9 0.0 all-gather.6.cloned.1.call-start
  7.9 0.9 multiply_exponential_fusion
  8.9 0.1 copy.10
  9.0 4.6 %mul.30 = f32[512,64,128]{2,1,0:T(8,128)S(1)} broadcast(f32[512,64]{1,0:T(8,128)S(1)} %copy.10), dimensions={0,1} | broadcast | bytes 16908288 | tf_op jit(solution)/shard_map/mul | solution.py:15
  13.6 18.3 %fusion = (bf16[512,8192]{1,0:T(8,128)(2,1)}, bf16[512,8192]{1,0:T(8,128)(2,1)}) fusion(f32[64,8,64,128]{3,2,1,0:T(8,128)S(1)} %bitcast.34, bf16[2,512,8192]{2,1,0:T(8,128)(2,1)} %param.5), kind=kLoop, calls=%fused_computation.2 | loop fusion | flops 25165824 | bytes 50331648 | tf_op jit(solution)/shard_map/convert_element_type | solution.py:16
  32.0 35.8 %all-gather.4.cloned.1.call-done = bf16[2,8192,128]{1,2,0:T(8,128)(2,1)} async-done(((bf16[2,8192,8]{1,2,0:T(8,128)(2,1)}), bf16[2,8192,128]{1,2,0:T(8,128)(2,1)}) %all-gather.4.cloned.1.call-update) | async-done | bytes 4194320 | tf_op jit(solution)/shard_map/all_gather | solution.py:25
  67.7 0.0 copy-start
  67.7 4.1 %slice_bitcast_fusion.1 = (bf16[8192,128]{0,1:T(8,128)(2,1)S(1)}, bf16[8192,128]{0,1:T(8,128)(2,1)}) fusion(bf16[2,8192,128]{1,2,0:T(8,128)(2,1)} %all-gather.4.cloned.1.call-done), kind=kLoop, calls=%fused_computation.13 | loop fusion | bytes 8388608 | tf_op jit(solution)/shard_map/squeeze | solution.py:27
  71.8 1.3 copy-done
  73.1 0.0 copy-start.2
  73.1 0.0 copy-start.3
  73.1 0.0 copy-start.1
  73.1 9.5 %fusion.2 = f32[1024,256]{1,0:T(8,128)} fusion(bf16[512,8192]{1,0:T(8,128)(2,1)} %get-tuple-element.7, bf16[512,8192]{1,0:T(8,128)(2,1)S(1)} %copy-done, bf16[8192,128]{0,1:T(8,128)(2,1)} %get-tuple-element.9, bf16[8192,128]{0,1:T(8,128)(2,1)S(1)} %get-tuple-element.8), kind=kOutput, calls=%fused_computation.8 | convolution fusion | flops 4336910336 | bytes 22020096 | tf_op jit(solution)/shard_map/dot_general | solution.py:28
  82.7 1.2 fusion.7
  83.9 0.8 pad_maximum_fusion.5
  84.7 0.0 all-gather.6.cloned.1.call-update
  84.8 0.0 copy-done.2
  84.8 0.0 copy-done.3
  84.8 0.6 dynamic-slice
  86.1 87.7 %all-gather.6.cloned.1.call-done = f32[16,512,128]{2,1,0:T(8,128)} async-done(((f32[2,512,128]{2,1,0:T(8,128)}), f32[16,512,128]{2,1,0:T(8,128)}) %all-gather.6.cloned.1.call-update) | async-done | bytes 4194320 | tf_op jit(solution)/shard_map/all_gather | solution.py:35
  173.8 2.4 reduce_sum.9
  176.2 0.0 copy-done.1
  176.3 0.0 slice-start
  176.3 0.0 slice-start.2
  176.3 0.1 multiply_convert_fusion
  176.5 0.0 slice-start.1
  176.5 0.0 slice-start.3
  176.5 10.0 %convolution_bitcast_fusion.1 = f32[1,8192,128]{2,1,0:T(8,128)} fusion(bf16[512,8192]{1,0:T(8,128)(2,1)} %get-tuple-element.7, bf16[512,8192]{1,0:T(8,128)(2,1)} %get-tuple-element.6, bf16[512,128]{1,0:T(8,128)(2,1)S(1)} %get-tuple-element.13, bf16[512,128]{1,0:T(8,128)(2,1)S(1)} %get-tuple-element.12), kind=kOutput, calls=%fused_computation.6 | convolution fusion | flops 2181562368 | bytes 21233664 | tf_op jit(solution)/shard_map/dot_general | solution.py:41
  186.5 0.0 slice-done
  186.5 0.0 slice-done.2
  186.5 0.8 slice-done.1
  187.3 1.2 slice-done.3
  188.5 6.3 %convolution_bitcast_fusion = f32[1,8192,128]{2,1,0:T(8,128)} fusion(bf16[512,8192]{1,0:T(8,128)(2,1)S(1)} %bitcast.38, bf16[512,8192]{1,0:T(8,128)(2,1)S(1)} %bitcast.36, bf16[512,128]{1,0:T(8,128)(2,1)S(1)} %fusion.17, bf16[512,128]{1,0:T(8,128)(2,1)S(1)} %get-tuple-element.13), kind=kOutput, calls=%fused_computation.5 | convolution fusion | flops 2181562368 | bytes 21233664 | tf_op jit(solution)/shard_map/dot_general | solution.py:44
  194.8 7.2 %pad_maximum_fusion.1 = f32[2,8192,128]{2,1,0:T(8,128)} fusion(f32[1,8192,128]{2,1,0:T(8,128)} %convolution_bitcast_fusion, f32[1,8192,128]{2,1,0:T(8,128)} %convolution_bitcast_fusion.1), kind=kLoop, calls=%fused_computation.7 | loop fusion | flops 2097152 | bytes 16777216 | tf_op jit(solution)/shard_map/stack | solution.py:48
  202.0 13.2 %copy.11 = f32[2,8192,128]{1,0,2:T(2,128)} copy(f32[2,8192,128]{2,1,0:T(8,128)} %pad_maximum_fusion.1) | data formatting | bytes 16777216 | tf_op jit(solution)/shard_map/stack | solution.py:48
  215.3 106.0 %all-reduce.2 = bf16[2,8192,128]{1,0,2:T(2,128)(2,1)} all-reduce(f32[2,8192,128]{1,0,2:T(2,128)} %copy.11), channel_id=3, replica_groups=mesh['rcv'=16,'src'=8] {'rcv'}, use_global_device_ids=true, to_apply=%region_1.0.clone | all-reduce | flops 2097152 | bytes 12582912
  321.3 1.1 dynamic-slice_convert_fusion
  322.4 0.9 copy.13
  323.3 0.1 constant_dynamic-slice_fusion
  323.4 0.7 copy.12
  (5 shorter events, 0.0 us)
Async XLA Ops:
  7.2 60.6 %all-gather.4.cloned.1.call-start = ((), (), s32[]{:S(2)}) async-start(), calls=%async_computation | async-start | bytes 4456448 | tf_op jit(solution)/shard_map/all_gather | solution.py:25
  7.9 165.9 %all-gather.6.cloned.1.call-start = ((), (), s32[]{:S(2)}) async-start(), calls=%async_computation.1 | async-start | bytes 4718592 | tf_op jit(solution)/shard_map/all_gather | solution.py:35
  67.7 5.4 %copy-start = (bf16[512,8192]{1,0:T(8,128)(2,1)S(1)}, bf16[512,8192]{1,0:T(8,128)(2,1)}, u32[]{:S(2)}) copy-start(bf16[512,8192]{1,0:T(8,128)(2,1)} %get-tuple-element.6) | copy-start | bytes 25165828
  73.1 11.7 %copy-start.2 = (s32[512]{0:T(512)S(1)}, s32[512]{0:T(512)}, u32[]{:S(2)}) copy-start(s32[512]{0:T(512)} %param.9) | copy-start | bytes 6148
  73.1 11.7 %copy-start.3 = (u32[128]{0:T(128)S(1)}, u32[128]{0:T(128)}, u32[]{:S(2)}) copy-start(u32[128]{0:T(128)} %constant.17) | copy-start | bytes 1540
  73.1 103.1 %copy-start.1 = (bf16[2,512,128]{2,1,0:T(8,128)(2,1)S(1)}, bf16[2,512,128]{2,1,0:T(8,128)(2,1)}, u32[]{:S(2)}) copy-start(bf16[2,512,128]{2,1,0:T(8,128)(2,1)} %param.8) | copy-start | bytes 786436
  176.3 10.2 %slice-start = ((s8[8388608]{0:T(1024)(128)(4,1)}), s8[4194304]{0:T(1024)(128)(4,1)S(1)}, s32[]{:S(2)}) async-start(s8[8388608]{0:T(1024)(128)(4,1)} %bitcast.35), calls=%async_computation.2 | async-start | bytes 8388608
  176.3 10.2 %slice-start.2 = ((s8[8388608]{0:T(1024)(128)(4,1)}), s8[4194304]{0:T(1024)(128)(4,1)S(1)}, s32[]{:S(2)}) async-start(s8[8388608]{0:T(1024)(128)(4,1)} %bitcast.37), calls=%async_computation.4 | async-start | bytes 8388608
  176.5 10.8 %slice-start.1 = ((s8[8388608]{0:T(1024)(128)(4,1)}), s8[4194304]{0:T(1024)(128)(4,1)S(1)}, s32[]{:S(2)}) async-start(s8[8388608]{0:T(1024)(128)(4,1)} %bitcast.35), calls=%async_computation.3 | async-start | bytes 8388608
  176.5 12.0 %slice-start.3 = ((s8[8388608]{0:T(1024)(128)(4,1)}), s8[4194304]{0:T(1024)(128)(4,1)S(1)}, s32[]{:S(2)}) async-start(s8[8388608]{0:T(1024)(128)(4,1)} %bitcast.37), calls=%async_computation.5 | async-start | bytes 8388608
Sparse Core Ops, SparseCore 0:
  10.5 57.1 all-gather.3
  84.9 88.8 all-gather.5
